TPU v7x, 32 devices: a whole 2x2x4 slice. The times are simulated.
32 devices in a mesh: span: 2 (over y), tmpl: 2 (over x), stn: 8 (over z, core).
Axes of the slice: x: 2, y: 2, z: 4, core: 2. Of those that a mesh axis runs over, the one named last changes fastest.
Arguments:
- signal: bfloat16 [3072, 8192], P('stn', ('span', 'tmpl')), parts along dimension 1, may hold values from -110 to 110
- waveforms: bfloat16 [16, 4, 8, 300], P('tmpl'), may hold values from -40 to 40
- station_groups: int32 [16, 4], P('tmpl'), may hold values from 0 to 7, all different within a row; in each aligned block of 8 rows (0 to 7, 8 to 15, ...) at most 8 rows name the same one
- channel_offsets: int32 [16, 4, 8], P('tmpl'), may hold values from 0 to 383
- moveouts: int32 [16, 4, 8], P('tmpl'), may hold values from 0 to 639
Outputs:
- stack: float32 [16, 6144], P(('tmpl', 'stn'), 'span'), parts along dimension 1
There are 2 independent parts, one for each index of `span`. A program takes and returns all parts, laid end to end along the dimension named above; an argument that names none is the same for every part. Nothing has to cross between parts.
Inputs may be any that keep to these rules, and one draw needn't show every extreme that they name: `station_groups`: A template's 4 station groups are distinct. Among the 8 templates of one index of tmpl, at most 8 touch any one station group, and in every draw some station group is touched by exactly 8 of them.
All inputs are finite; a program needn't handle non-finite values.
Results may differ from a plain program's by a relative error of at most 0.0003.
Values may be sent and summed in bfloat16 or wider, within the bound.
No kernel may reach another device: no remote copies, remote signals or barrier semaphores. Data moves between devices by JAX's collectives and lax.ppermute only.
A program may use at most 64 MiB of HBM per device.

v0:
```python
import jax
import jax.numpy as jnp
from jax import lax
from jax.sharding import PartitionSpec as P

L = 300
NT = 3072
eps_value = 1e-05


def toeplitz_tiles(wave):
    length = wave.shape[0]
    padded = jnp.concatenate(
        [jnp.zeros((128,), wave.dtype), wave, jnp.zeros((513 - length,), wave.dtype)]
    )
    repeated = jnp.tile(padded, 128)[: 128 * 640].reshape(128, 640)
    return repeated[:, 128:640]


def entry_stack(wave_rows, chan_rows, move_rows, series, rms_data):
    toeplitz = jax.vmap(toeplitz_tiles)(wave_rows)
    blocks = NT // 128

    def one_slot(channel, lag_shift):
        data_row = lax.dynamic_slice(series, (channel, lag_shift), (1, NT + 384))
        energy = lax.dynamic_slice(rms_data, (channel, lag_shift), (1, NT))
        return (data_row.reshape(blocks + 3, 128), energy.reshape(NT))

    segments, scales = jax.vmap(one_slot)(chan_rows, move_rows)
    correl = jnp.zeros((wave_rows.shape[0], blocks, 128), jnp.float32)
    for offset in range(4):
        correl = correl + jnp.einsum(
            "pac,pbc->pab",
            segments[:, offset : offset + blocks],
            toeplitz[:, :, offset * 128 : (offset + 1) * 128],
            preferred_element_type=jnp.float32,
        )
    waves_wide = wave_rows.astype(jnp.float32)
    wave_rms = jnp.sqrt(jnp.mean(waves_wide * waves_wide, axis=1) + eps_value)
    normed = correl.reshape(wave_rows.shape[0], NT) / (L * wave_rms[:, None] * scales)
    return jnp.sum(normed, axis=0)


def add_sources(received):
    return jnp.sum(received, axis=0)


def shards(signal, waveforms, station_groups, channel_offsets, moveouts):
    series = lax.all_gather(signal, "tmpl", axis=1, tiled=True)
    group_rows = waveforms.shape[0]
    touch_count = station_groups.shape[1]
    station_count = lax.axis_size("stn")
    own_rows = group_rows // station_count
    capacity = min(group_rows, 2 * group_rows * touch_count // station_count)
    station = lax.axis_index("stn")
    is_local = station_groups == station
    present = jnp.any(is_local, axis=1)
    touch_pick = jnp.sum(
        is_local.astype(jnp.int32) * jnp.arange(touch_count, dtype=jnp.int32)[None, :], axis=1
    )
    position = jnp.cumsum(present.astype(jnp.int32)) - 1
    target = jnp.where(present, position, capacity)
    entry_tpl = (
        jnp.zeros((capacity,), jnp.int32)
        .at[target]
        .set(jnp.arange(group_rows, dtype=jnp.int32), mode="drop")
    )
    entry_touch = touch_pick[entry_tpl]
    live_count = jnp.sum(present.astype(jnp.int32))
    is_live = jnp.arange(capacity, dtype=jnp.int32) < live_count
    wave_sel = waveforms[entry_tpl, entry_touch]
    chan_sel = channel_offsets[entry_tpl, entry_touch]
    move_sel = moveouts[entry_tpl, entry_touch]
    wide_series = series.astype(jnp.float32)
    squares = wide_series * wide_series
    running = jnp.concatenate(
        [jnp.zeros((series.shape[0], 1), jnp.float32), jnp.cumsum(squares, axis=1)], axis=1
    )
    windows = running[:, L:] - running[:, :-L]
    rms_data = jnp.sqrt(windows / L + eps_value)

    def run_entry(entry_num):
        stacked = entry_stack(
            wave_sel[entry_num], chan_sel[entry_num], move_sel[entry_num], series, rms_data
        )
        return jnp.where(is_live[entry_num], stacked, 0.0)

    stacks = lax.map(run_entry, jnp.arange(capacity, dtype=jnp.int32))
    partial_sum = jnp.zeros((group_rows, NT), jnp.float32).at[entry_tpl].add(stacks)
    by_owner = partial_sum.reshape(station_count, own_rows, NT)
    return add_sources(lax.all_to_all(by_owner, "stn", split_axis=0, concat_axis=0, tiled=True))


def solution(mesh):
    in_specs = (
        P("stn", ("span", "tmpl")),
        P("tmpl", None, None, None),
        P("tmpl", None),
        P("tmpl", None, None),
        P("tmpl", None, None),
    )
    out_specs = P(("tmpl", "stn"), "span")
    return jax.shard_map(shards, mesh=mesh, in_specs=in_specs, out_specs=out_specs, check_vma=False)
```

profile of v0, /device:TPU:0, one launch (start us, length us, event | category | flops | bytes accessed | tf_op | source)
XLA Modules:
  0.0 578.0 jit_solution(9084490409785776008)
XLA Ops:
  14.1 42.4 %all-gather.2.cloned.1.call-done = bf16[384,4096]{1,0:T(8,128)(2,1)} async-done(((bf16[384,2048]{1,0:T(8,128)(2,1)}), bf16[384,4096]{1,0:T(8,128)(2,1)}) %all-gather.2.cloned.1.call-update) | async-done | bytes 3145744 | tf_op jit(solution)/shard_map/all_gather | solution.py:49
  56.5 2.6 multiply_bitcast_fusion
  59.2 3.9 copy.30
  63.1 6.7 %copy.20 = f32[384,32,128]{0,1,2:T(8,128)} copy(f32[384,32,128]{2,1,0:T(8,128)} %bitcast.101) | data formatting | bytes 12582912 | tf_op jit(solution)/shard_map/reshape.2
  69.9 3.2 fusion.29
  73.1 2.7 copy-done.1
  75.8 3.5 broadcast_add_fusion
  79.3 3.6 copy.21
  83.0 5.2 fusion.16
  88.1 6.5 %copy.22 = f32[384,3797]{1,0:T(8,128)} copy(f32[384,3797]{0,1:T(8,128)} %fusion.16) | data formatting | bytes 11664384 | tf_op jit(solution)/shard_map/while | solution.py:88
  94.6 464.3 %while.21 = (s32[]{:T(128)}, f32[8,3072]{1,0:T(8,128)S(1)}, s32[8]{0:T(128)S(1)}, pred[8]{0:T(512)(128)(4,1)S(1)}, s32[8,8]{1,0:T(8,128)S(1)}, /*index=5*/s32[8,...) while((s32[]{:T(128)}, f32[8,3072]{1,0:T(8,128)S(1)}, ...), condition=%wide.region_10.11_spmd.clone, body=%wide.region_7.10_spmd.sunk.clone | while | flops 25351368 | bytes 14289844 | solution.py:88
  97.4 24.5 %while.19 = (s32[]{:T(128)}, bf16[384,4096]{1,0:T(8,128)(2,1)}, s32[8,2]{0,1:T(2,128)S(1)}, bf16[8,1,3456]{2,0,1:T(8,128)(2,1)S(1)}, s32[]{:T(128)}, /*index=5*/s32[]{:T(128)}) while((s32[]{:T(128)}, bf16[384,4096]{1,0:T(8,128)(2,1)}, s32[8,2]{0,1:T(2,128)S(1)}, bf16[8,1,3456]{2,0,1:T(8,128)(2,1)S(1)}, s32[]{:T(128)}, /*index=5*/s32[]{:T(128)}) %tuple.81), condition=%wide.while_cond, body=%wide.while_body.sunk | while | flops 2 | bytes 27765 | solution.py:25
  122.3 2.3 reshape.276
  127.1 23.6 %while.20 = (s32[]{:T(128)}, f32[384,3797]{1,0:T(8,128)}, s32[8,2]{0,1:T(2,128)S(1)}, f32[8,1,3072]{2,1,0:T(1,128)S(1)}, s32[]{:T(128)}) while((s32[]{:T(128)}, f32[384,3797]{1,0:T(8,128)}, s32[8,2]{0,1:T(2,128)S(1)}, f32[8,1,3072]{2,1,0:T(1,128)S(1)}, s32[]{:T(128)}) %tuple.84), condition=%wide.while_cond.1, body=%wide.while_body.1.sunk | while | flops 2 | bytes 24685 | solution.py:26
  127.8 2.3 bitcast_dynamic-update-slice_fusion.2
  130.7 2.3 bitcast_dynamic-update-slice_fusion.2
  133.7 2.3 bitcast_dynamic-update-slice_fusion.2
  136.6 2.3 bitcast_dynamic-update-slice_fusion.2
  139.6 2.3 bitcast_dynamic-update-slice_fusion.2
  142.5 2.3 bitcast_dynamic-update-slice_fusion.2
  145.5 2.3 bitcast_dynamic-update-slice_fusion.2
  155.5 24.5 %while.19 = (s32[]{:T(128)}, bf16[384,4096]{1,0:T(8,128)(2,1)}, s32[8,2]{0,1:T(2,128)S(1)}, bf16[8,1,3456]{2,0,1:T(8,128)(2,1)S(1)}, s32[]{:T(128)}, /*index=5*/s32[]{:T(128)}) while((s32[]{:T(128)}, bf16[384,4096]{1,0:T(8,128)(2,1)}, s32[8,2]{0,1:T(2,128)S(1)}, bf16[8,1,3456]{2,0,1:T(8,128)(2,1)S(1)}, s32[]{:T(128)}, /*index=5*/s32[]{:T(128)}) %tuple.81), condition=%wide.while_cond, body=%wide.while_body.sunk | while | flops 2 | bytes 27765 | solution.py:25
  180.4 2.3 reshape.276
  185.1 23.6 %while.20 = (s32[]{:T(128)}, f32[384,3797]{1,0:T(8,128)}, s32[8,2]{0,1:T(2,128)S(1)}, f32[8,1,3072]{2,1,0:T(1,128)S(1)}, s32[]{:T(128)}) while((s32[]{:T(128)}, f32[384,3797]{1,0:T(8,128)}, s32[8,2]{0,1:T(2,128)S(1)}, f32[8,1,3072]{2,1,0:T(1,128)S(1)}, s32[]{:T(128)}) %tuple.84), condition=%wide.while_cond.1, body=%wide.while_body.1.sunk | while | flops 2 | bytes 24685 | solution.py:26
  188.8 2.3 bitcast_dynamic-update-slice_fusion.2
  197.6 2.3 bitcast_dynamic-update-slice_fusion.2
  200.6 2.3 bitcast_dynamic-update-slice_fusion.2
  213.5 24.5 %while.19 = (s32[]{:T(128)}, bf16[384,4096]{1,0:T(8,128)(2,1)}, s32[8,2]{0,1:T(2,128)S(1)}, bf16[8,1,3456]{2,0,1:T(8,128)(2,1)S(1)}, s32[]{:T(128)}, /*index=5*/s32[]{:T(128)}) while((s32[]{:T(128)}, bf16[384,4096]{1,0:T(8,128)(2,1)}, s32[8,2]{0,1:T(2,128)S(1)}, bf16[8,1,3456]{2,0,1:T(8,128)(2,1)S(1)}, s32[]{:T(128)}, /*index=5*/s32[]{:T(128)}) %tuple.81), condition=%wide.while_cond, body=%wide.while_body.sunk | while | flops 2 | bytes 27765 | solution.py:25
  238.4 2.3 reshape.276
  243.2 23.6 %while.20 = (s32[]{:T(128)}, f32[384,3797]{1,0:T(8,128)}, s32[8,2]{0,1:T(2,128)S(1)}, f32[8,1,3072]{2,1,0:T(1,128)S(1)}, s32[]{:T(128)}) while((s32[]{:T(128)}, f32[384,3797]{1,0:T(8,128)}, s32[8,2]{0,1:T(2,128)S(1)}, f32[8,1,3072]{2,1,0:T(1,128)S(1)}, s32[]{:T(128)}) %tuple.84), condition=%wide.while_cond.1, body=%wide.while_body.1.sunk | while | flops 2 | bytes 24685 | solution.py:26
  243.9 2.3 bitcast_dynamic-update-slice_fusion.2
  252.7 2.3 bitcast_dynamic-update-slice_fusion.2
  255.7 2.3 bitcast_dynamic-update-slice_fusion.2
  264.5 2.3 bitcast_dynamic-update-slice_fusion.2
  271.5 24.5 %while.19 = (s32[]{:T(128)}, bf16[384,4096]{1,0:T(8,128)(2,1)}, s32[8,2]{0,1:T(2,128)S(1)}, bf16[8,1,3456]{2,0,1:T(8,128)(2,1)S(1)}, s32[]{:T(128)}, /*index=5*/s32[]{:T(128)}) while((s32[]{:T(128)}, bf16[384,4096]{1,0:T(8,128)(2,1)}, s32[8,2]{0,1:T(2,128)S(1)}, bf16[8,1,3456]{2,0,1:T(8,128)(2,1)S(1)}, s32[]{:T(128)}, /*index=5*/s32[]{:T(128)}) %tuple.81), condition=%wide.while_cond, body=%wide.while_body.sunk | while | flops 2 | bytes 27765 | solution.py:25
  296.5 2.3 reshape.276
  301.2 23.6 %while.20 = (s32[]{:T(128)}, f32[384,3797]{1,0:T(8,128)}, s32[8,2]{0,1:T(2,128)S(1)}, f32[8,1,3072]{2,1,0:T(1,128)S(1)}, s32[]{:T(128)}) while((s32[]{:T(128)}, f32[384,3797]{1,0:T(8,128)}, s32[8,2]{0,1:T(2,128)S(1)}, f32[8,1,3072]{2,1,0:T(1,128)S(1)}, s32[]{:T(128)}) %tuple.84), condition=%wide.while_cond.1, body=%wide.while_body.1.sunk | while | flops 2 | bytes 24685 | solution.py:26
  307.8 2.3 bitcast_dynamic-update-slice_fusion.2
  310.8 2.3 bitcast_dynamic-update-slice_fusion.2
  319.6 2.3 bitcast_dynamic-update-slice_fusion.2
  329.6 24.5 %while.19 = (s32[]{:T(128)}, bf16[384,4096]{1,0:T(8,128)(2,1)}, s32[8,2]{0,1:T(2,128)S(1)}, bf16[8,1,3456]{2,0,1:T(8,128)(2,1)S(1)}, s32[]{:T(128)}, /*index=5*/s32[]{:T(128)}) while((s32[]{:T(128)}, bf16[384,4096]{1,0:T(8,128)(2,1)}, s32[8,2]{0,1:T(2,128)S(1)}, bf16[8,1,3456]{2,0,1:T(8,128)(2,1)S(1)}, s32[]{:T(128)}, /*index=5*/s32[]{:T(128)}) %tuple.81), condition=%wide.while_cond, body=%wide.while_body.sunk | while | flops 2 | bytes 27765 | solution.py:25
  354.5 2.3 reshape.276
  359.3 23.6 %while.20 = (s32[]{:T(128)}, f32[384,3797]{1,0:T(8,128)}, s32[8,2]{0,1:T(2,128)S(1)}, f32[8,1,3072]{2,1,0:T(1,128)S(1)}, s32[]{:T(128)}) while((s32[]{:T(128)}, f32[384,3797]{1,0:T(8,128)}, s32[8,2]{0,1:T(2,128)S(1)}, f32[8,1,3072]{2,1,0:T(1,128)S(1)}, s32[]{:T(128)}) %tuple.84), condition=%wide.while_cond.1, body=%wide.while_body.1.sunk | while | flops 2 | bytes 24685 | solution.py:26
  362.9 2.3 bitcast_dynamic-update-slice_fusion.2
  365.8 2.3 bitcast_dynamic-update-slice_fusion.2
  374.7 2.3 bitcast_dynamic-update-slice_fusion.2
  387.6 24.5 %while.19 = (s32[]{:T(128)}, bf16[384,4096]{1,0:T(8,128)(2,1)}, s32[8,2]{0,1:T(2,128)S(1)}, bf16[8,1,3456]{2,0,1:T(8,128)(2,1)S(1)}, s32[]{:T(128)}, /*index=5*/s32[]{:T(128)}) while((s32[]{:T(128)}, bf16[384,4096]{1,0:T(8,128)(2,1)}, s32[8,2]{0,1:T(2,128)S(1)}, bf16[8,1,3456]{2,0,1:T(8,128)(2,1)S(1)}, s32[]{:T(128)}, /*index=5*/s32[]{:T(128)}) %tuple.81), condition=%wide.while_cond, body=%wide.while_body.sunk | while | flops 2 | bytes 27765 | solution.py:25
  412.6 2.3 reshape.276
  417.3 23.6 %while.20 = (s32[]{:T(128)}, f32[384,3797]{1,0:T(8,128)}, s32[8,2]{0,1:T(2,128)S(1)}, f32[8,1,3072]{2,1,0:T(1,128)S(1)}, s32[]{:T(128)}) while((s32[]{:T(128)}, f32[384,3797]{1,0:T(8,128)}, s32[8,2]{0,1:T(2,128)S(1)}, f32[8,1,3072]{2,1,0:T(1,128)S(1)}, s32[]{:T(128)}) %tuple.84), condition=%wide.while_cond.1, body=%wide.while_body.1.sunk | while | flops 2 | bytes 24685 | solution.py:26
  418.0 2.3 bitcast_dynamic-update-slice_fusion.2
  420.9 2.3 bitcast_dynamic-update-slice_fusion.2
  429.8 2.3 bitcast_dynamic-update-slice_fusion.2
  445.7 24.5 %while.19 = (s32[]{:T(128)}, bf16[384,4096]{1,0:T(8,128)(2,1)}, s32[8,2]{0,1:T(2,128)S(1)}, bf16[8,1,3456]{2,0,1:T(8,128)(2,1)S(1)}, s32[]{:T(128)}, /*index=5*/s32[]{:T(128)}) while((s32[]{:T(128)}, bf16[384,4096]{1,0:T(8,128)(2,1)}, s32[8,2]{0,1:T(2,128)S(1)}, bf16[8,1,3456]{2,0,1:T(8,128)(2,1)S(1)}, s32[]{:T(128)}, /*index=5*/s32[]{:T(128)}) %tuple.81), condition=%wide.while_cond, body=%wide.while_body.sunk | while | flops 2 | bytes 27765 | solution.py:25
  470.6 2.3 reshape.276
  475.3 23.6 %while.20 = (s32[]{:T(128)}, f32[384,3797]{1,0:T(8,128)}, s32[8,2]{0,1:T(2,128)S(1)}, f32[8,1,3072]{2,1,0:T(1,128)S(1)}, s32[]{:T(128)}) while((s32[]{:T(128)}, f32[384,3797]{1,0:T(8,128)}, s32[8,2]{0,1:T(2,128)S(1)}, f32[8,1,3072]{2,1,0:T(1,128)S(1)}, s32[]{:T(128)}) %tuple.84), condition=%wide.while_cond.1, body=%wide.while_body.1.sunk | while | flops 2 | bytes 24685 | solution.py:26
  476.0 2.3 bitcast_dynamic-update-slice_fusion.2
  484.9 2.3 bitcast_dynamic-update-slice_fusion.2
  496.7 2.3 bitcast_dynamic-update-slice_fusion.2
  503.7 24.5 %while.19 = (s32[]{:T(128)}, bf16[384,4096]{1,0:T(8,128)(2,1)}, s32[8,2]{0,1:T(2,128)S(1)}, bf16[8,1,3456]{2,0,1:T(8,128)(2,1)S(1)}, s32[]{:T(128)}, /*index=5*/s32[]{:T(128)}) while((s32[]{:T(128)}, bf16[384,4096]{1,0:T(8,128)(2,1)}, s32[8,2]{0,1:T(2,128)S(1)}, bf16[8,1,3456]{2,0,1:T(8,128)(2,1)S(1)}, s32[]{:T(128)}, /*index=5*/s32[]{:T(128)}) %tuple.81), condition=%wide.while_cond, body=%wide.while_body.sunk | while | flops 2 | bytes 27765 | solution.py:25
  528.6 2.3 reshape.276
  533.4 23.6 %while.20 = (s32[]{:T(128)}, f32[384,3797]{1,0:T(8,128)}, s32[8,2]{0,1:T(2,128)S(1)}, f32[8,1,3072]{2,1,0:T(1,128)S(1)}, s32[]{:T(128)}) while((s32[]{:T(128)}, f32[384,3797]{1,0:T(8,128)}, s32[8,2]{0,1:T(2,128)S(1)}, f32[8,1,3072]{2,1,0:T(1,128)S(1)}, s32[]{:T(128)}) %tuple.84), condition=%wide.while_cond.1, body=%wide.while_body.1.sunk | while | flops 2 | bytes 24685 | solution.py:26
  540.0 2.3 bitcast_dynamic-update-slice_fusion.2
  551.8 2.3 bitcast_dynamic-update-slice_fusion.2
  559.8 10.7 %all_to_all.5 = f32[8,1,3072]{2,1,0:T(1,128)S(1)} all-to-all(f32[8,1,3072]{2,1,0:T(1,128)S(1)} %reshape.180), channel_id=1, replica_groups=mesh['span'=2,'tmpl'=2,'stn'=8] {'stn'}, dimensions={0} | all-to-all | bytes 196608 | tf_op jit(solution)/shard_map/all_to_all | solution.py:91
  (641 shorter events, 371.2 us)
Async XLA Ops:
  6.5 3.0 copy-start
  6.5 50.0 %all-gather.2.cloned.1.call-start = ((), (), s32[]{:S(2)}) async-start(), calls=%async_computation.1 | async-start | bytes 4718592 | tf_op jit(solution)/shard_map/all_gather | solution.py:49
  73.1 2.7 copy-start.1
Sparse Core Ops, SparseCore 0:
  8.9 47.6 all-gather.1
where the time goes:
time: 586 us; the launch traced here: 578 us
  local copies, waits for them, and re-layouts  457 us (78%)
  waiting for transfers between devices  43.2 us (7%)
  other arithmetic  25.2 us (4%)
  loops' own time  20.5 us (3%)
  between operations  13.5 us (2%)
  blocking collectives  10.7 us (2%)
  matrix products  8.11 us (1%)
    gather x448, local copies, waits for them, and re-layouts  382 us
    all_gather x1, waiting for transfers between devices, shards(): series = lax.all_gather(signal, 'tmpl', axis=1, tiled=True)  42.4 us
    while x16, local copies, waits for them, and re-layouts  19.7 us
    another operation x1, loops' own time, shards(): stacks = lax.map(run_entry, jnp.arange(capacity, dtype=jnp.int32))  17.7 us
    another operation x16, local copies, waits for them, and re-layouts, toeplitz_tiles(): repeated = jnp.tile(padded, 128)[:128 * 640].reshape(128, 640)  12.1 us
  transfers between devices with their start and end apart: 1, of which 1 were waited for; matrix products, arithmetic and copies ran while one was open for 1% of the time, Pallas kernels for 0%

commit v1 on v0

--- a/solution.py
+++ b/solution.py
@@ -1,3 +1,4 @@
+import functools
 import jax
 import jax.numpy as jnp
 from jax import lax
@@ -6,6 +7,26 @@
 L = 300
 NT = 3072
 eps_value = 1e-05
+
+
+def connect_map(local_x, row_axis, along_dim):
+    val2 = jax.lax.axis_size(row_axis)
+    reply = jax.lax.axis_index(row_axis)
+    tmp, vec_out = (val2, reply)
+    heard, low = (local_x, 1)
+    while low < tmp:
+        block_next = range(tmp)
+        long_array = map(lambda nth: (nth, nth ^ low), block_next)
+        piece_next = list(long_array)
+        new = jax.lax.ppermute(heard, axis_name=row_axis, perm=piece_next)
+        next_value = jnp.concatenate([heard, new], axis=along_dim)
+        after = jnp.concatenate([new, heard], axis=along_dim)
+        heard = jnp.where(vec_out & low == 0, next_value, after)
+        low = 2 * low
+    return heard
+
+
+figure_start = functools.partial(connect_map, row_axis="tmpl", along_dim=1)
 
 
 def toeplitz_tiles(wave):
@@ -46,7 +67,7 @@
 
 
 def shards(signal, waveforms, station_groups, channel_offsets, moveouts):
-    series = lax.all_gather(signal, "tmpl", axis=1, tiled=True)
+    series = figure_start(signal)
     group_rows = waveforms.shape[0]
     touch_count = station_groups.shape[1]
     station_count = lax.axis_size("stn")

time: 586 us -> 553 us (0.944)
  waiting for transfers between devices: 43.2 us -> 24.4 us
  between operations: 13.5 us -> 0.12 us
  local copies, waits for them, and re-layouts: 457 us -> 451 us
    all_gather x1 -> x0, waiting for transfers between devices: 42.4 us -> none  [shards(): series = lax.all_gather(signal, 'tmpl', axis=1, tiled=True)]
    ppermute x0 -> x1, waiting for transfers between devices: none -> 24.4 us  [connect_map(): new = jax.lax.ppermute(heard, axis_name=row_axis, perm=piece_next)]
    another operation x20 -> x19, local copies, waits for them, and re-layouts: 10.4 us -> 4.5 us
  transfers between devices with their start and end apart: 1 -> 1, of which waited for: 1 -> 1; matrix products, arithmetic and copies ran while one was open for 1% -> 2% of each run, Pallas kernels for 0% -> 0%
where the time goes in v1:
time: 553 us; the launch traced here: 545 us
  local copies, waits for them, and re-layouts  451 us (82%)
  other arithmetic  27.2 us (5%)
  waiting for transfers between devices  24.4 us (4%)
  loops' own time  20.5 us (4%)
  blocking collectives  11.2 us (2%)
  matrix products  8.1 us (1%)
    gather x448, local copies, waits for them, and re-layouts  380 us
    ppermute x1, waiting for transfers between devices, connect_map(): new = jax.lax.ppermute(heard, axis_name=row_axis, perm=piece_next)  24.4 us
    while x16, local copies, waits for them, and re-layouts  19.7 us
    another operation x1, loops' own time, shards(): stacks = lax.map(run_entry, jnp.arange(capacity, dtype=jnp.int32))  17.6 us
    another operation x16, local copies, waits for them, and re-layouts, toeplitz_tiles(): repeated = jnp.tile(padded, 128)[:128 * 640].reshape(128, 640)  12.1 us
    all_to_all x1, blocking collectives, shards(): lax.all_to_all(by_owner, 'stn', split_axis=0, concat_axis=0, tiled=True)  11.2 us
  transfers between devices with their start and end apart: 1, of which 1 were waited for; matrix products, arithmetic and copies ran while one was open for 2% of the time, Pallas kernels for 0%

profile of v1, /device:TPU:0, one launch (start us, length us, event | category | flops | bytes accessed | tf_op | source)
XLA Modules:
  0.0 545.3 jit_solution(13455923340178657508)
XLA Ops:
  0.0 3.0 collective-permute-start
  13.2 24.4 %collective-permute-done = bf16[384,2048]{1,0:T(8,128)(2,1)} collective-permute-done((bf16[384,2048]{1,0:T(8,128)(2,1)}, bf16[384,2048]{1,0:T(8,128)(2,1)}, u32[]{:S(2)}, u32[]{:S(2)}) %collective-permute-start) | collective-permute-done | bytes 1572896 | tf_op jit(solution)/shard_map/ppermute | solution.py:21
  37.7 3.0 copy.40
  40.7 2.6 copy.27
  43.3 3.6 fusion.13
  47.8 3.5 broadcast_add_fusion
  51.2 3.6 copy.30
  54.9 5.2 fusion.19
  60.1 6.6 %copy.31 = f32[384,3797]{1,0:T(8,128)} copy(f32[384,3797]{0,1:T(8,128)} %fusion.19) | data formatting | bytes 11664384 | tf_op jit(solution)/shard_map/while | solution.py:109
  66.7 4.2 maximum_select_fusion
  70.9 461.7 %while.21 = (s32[]{:T(128)}, f32[8,3072]{1,0:T(8,128)S(1)}, s32[8]{0:T(128)S(1)}, pred[8]{0:T(512)(128)(4,1)S(1)}, s32[8,8]{1,0:T(8,128)S(1)}, /*index=5*/s32[8,...) while((s32[]{:T(128)}, f32[8,3072]{1,0:T(8,128)S(1)}, ...), condition=%wide.region_10.11_spmd.clone, body=%wide.region_7.10_spmd.sunk.clone | while | flops 25351368 | bytes 14289844 | solution.py:109
  73.7 24.4 %while.19 = (s32[]{:T(128)}, bf16[384,4096]{1,0:T(8,128)(2,1)}, s32[8,2]{0,1:T(2,128)S(1)}, bf16[8,1,3456]{2,0,1:T(8,128)(2,1)S(1)}, s32[]{:T(128)}, /*index=5*/s32[]{:T(128)}) while((s32[]{:T(128)}, bf16[384,4096]{1,0:T(8,128)(2,1)}, s32[8,2]{0,1:T(2,128)S(1)}, bf16[8,1,3456]{2,0,1:T(8,128)(2,1)S(1)}, s32[]{:T(128)}, /*index=5*/s32[]{:T(128)}) %tuple.81), condition=%wide.while_cond, body=%wide.while_body.sunk | while | flops 2 | bytes 27765 | solution.py:46
  98.4 2.3 reshape.278
  103.2 23.5 %while.20 = (s32[]{:T(128)}, f32[384,3797]{1,0:T(8,128)}, s32[8,2]{0,1:T(2,128)S(1)}, f32[8,1,3072]{2,1,0:T(1,128)S(1)}, s32[]{:T(128)}) while((s32[]{:T(128)}, f32[384,3797]{1,0:T(8,128)}, s32[8,2]{0,1:T(2,128)S(1)}, f32[8,1,3072]{2,1,0:T(1,128)S(1)}, s32[]{:T(128)}) %tuple.84), condition=%wide.while_cond.1, body=%wide.while_body.1.sunk | while | flops 2 | bytes 24685 | solution.py:47
  103.9 2.2 bitcast_dynamic-update-slice_fusion.2
  106.8 2.2 bitcast_dynamic-update-slice_fusion.2
  109.7 2.2 bitcast_dynamic-update-slice_fusion.2
  112.7 2.2 bitcast_dynamic-update-slice_fusion.2
  115.6 2.2 bitcast_dynamic-update-slice_fusion.2
  118.5 2.2 bitcast_dynamic-update-slice_fusion.2
  121.5 2.2 bitcast_dynamic-update-slice_fusion.2
  124.4 2.2 bitcast_dynamic-update-slice_fusion.2
  131.4 24.4 %while.19 = (s32[]{:T(128)}, bf16[384,4096]{1,0:T(8,128)(2,1)}, s32[8,2]{0,1:T(2,128)S(1)}, bf16[8,1,3456]{2,0,1:T(8,128)(2,1)S(1)}, s32[]{:T(128)}, /*index=5*/s32[]{:T(128)}) while((s32[]{:T(128)}, bf16[384,4096]{1,0:T(8,128)(2,1)}, s32[8,2]{0,1:T(2,128)S(1)}, bf16[8,1,3456]{2,0,1:T(8,128)(2,1)S(1)}, s32[]{:T(128)}, /*index=5*/s32[]{:T(128)}) %tuple.81), condition=%wide.while_cond, body=%wide.while_body.sunk | while | flops 2 | bytes 27765 | solution.py:46
  156.1 2.3 reshape.278
  160.9 23.5 %while.20 = (s32[]{:T(128)}, f32[384,3797]{1,0:T(8,128)}, s32[8,2]{0,1:T(2,128)S(1)}, f32[8,1,3072]{2,1,0:T(1,128)S(1)}, s32[]{:T(128)}) while((s32[]{:T(128)}, f32[384,3797]{1,0:T(8,128)}, s32[8,2]{0,1:T(2,128)S(1)}, f32[8,1,3072]{2,1,0:T(1,128)S(1)}, s32[]{:T(128)}) %tuple.84), condition=%wide.while_cond.1, body=%wide.while_body.1.sunk | while | flops 2 | bytes 24685 | solution.py:47
  164.5 2.2 bitcast_dynamic-update-slice_fusion.2
  167.4 2.2 bitcast_dynamic-update-slice_fusion.2
  170.4 2.2 bitcast_dynamic-update-slice_fusion.2
  173.3 2.2 bitcast_dynamic-update-slice_fusion.2
  176.2 2.2 bitcast_dynamic-update-slice_fusion.2
  179.2 2.2 bitcast_dynamic-update-slice_fusion.2
  182.1 2.2 bitcast_dynamic-update-slice_fusion.2
  189.1 24.4 %while.19 = (s32[]{:T(128)}, bf16[384,4096]{1,0:T(8,128)(2,1)}, s32[8,2]{0,1:T(2,128)S(1)}, bf16[8,1,3456]{2,0,1:T(8,128)(2,1)S(1)}, s32[]{:T(128)}, /*index=5*/s32[]{:T(128)}) while((s32[]{:T(128)}, bf16[384,4096]{1,0:T(8,128)(2,1)}, s32[8,2]{0,1:T(2,128)S(1)}, bf16[8,1,3456]{2,0,1:T(8,128)(2,1)S(1)}, s32[]{:T(128)}, /*index=5*/s32[]{:T(128)}) %tuple.81), condition=%wide.while_cond, body=%wide.while_body.sunk | while | flops 2 | bytes 27765 | solution.py:46
  213.9 2.3 reshape.278
  218.6 23.5 %while.20 = (s32[]{:T(128)}, f32[384,3797]{1,0:T(8,128)}, s32[8,2]{0,1:T(2,128)S(1)}, f32[8,1,3072]{2,1,0:T(1,128)S(1)}, s32[]{:T(128)}) while((s32[]{:T(128)}, f32[384,3797]{1,0:T(8,128)}, s32[8,2]{0,1:T(2,128)S(1)}, f32[8,1,3072]{2,1,0:T(1,128)S(1)}, s32[]{:T(128)}) %tuple.84), condition=%wide.while_cond.1, body=%wide.while_body.1.sunk | while | flops 2 | bytes 24685 | solution.py:47
  219.3 2.2 bitcast_dynamic-update-slice_fusion.2
  222.2 2.2 bitcast_dynamic-update-slice_fusion.2
  225.2 2.2 bitcast_dynamic-update-slice_fusion.2
  228.1 2.2 bitcast_dynamic-update-slice_fusion.2
  231.0 2.2 bitcast_dynamic-update-slice_fusion.2
  234.0 2.2 bitcast_dynamic-update-slice_fusion.2
  236.9 2.2 bitcast_dynamic-update-slice_fusion.2
  246.8 24.4 %while.19 = (s32[]{:T(128)}, bf16[384,4096]{1,0:T(8,128)(2,1)}, s32[8,2]{0,1:T(2,128)S(1)}, bf16[8,1,3456]{2,0,1:T(8,128)(2,1)S(1)}, s32[]{:T(128)}, /*index=5*/s32[]{:T(128)}) while((s32[]{:T(128)}, bf16[384,4096]{1,0:T(8,128)(2,1)}, s32[8,2]{0,1:T(2,128)S(1)}, bf16[8,1,3456]{2,0,1:T(8,128)(2,1)S(1)}, s32[]{:T(128)}, /*index=5*/s32[]{:T(128)}) %tuple.81), condition=%wide.while_cond, body=%wide.while_body.sunk | while | flops 2 | bytes 27765 | solution.py:46
  271.6 2.3 reshape.278
  276.3 23.5 %while.20 = (s32[]{:T(128)}, f32[384,3797]{1,0:T(8,128)}, s32[8,2]{0,1:T(2,128)S(1)}, f32[8,1,3072]{2,1,0:T(1,128)S(1)}, s32[]{:T(128)}) while((s32[]{:T(128)}, f32[384,3797]{1,0:T(8,128)}, s32[8,2]{0,1:T(2,128)S(1)}, f32[8,1,3072]{2,1,0:T(1,128)S(1)}, s32[]{:T(128)}) %tuple.84), condition=%wide.while_cond.1, body=%wide.while_body.1.sunk | while | flops 2 | bytes 24685 | solution.py:47
  277.0 2.2 bitcast_dynamic-update-slice_fusion.2
  279.9 2.2 bitcast_dynamic-update-slice_fusion.2
  282.9 2.2 bitcast_dynamic-update-slice_fusion.2
  285.8 2.2 bitcast_dynamic-update-slice_fusion.2
  288.7 2.2 bitcast_dynamic-update-slice_fusion.2
  291.7 2.2 bitcast_dynamic-update-slice_fusion.2
  304.5 24.4 %while.19 = (s32[]{:T(128)}, bf16[384,4096]{1,0:T(8,128)(2,1)}, s32[8,2]{0,1:T(2,128)S(1)}, bf16[8,1,3456]{2,0,1:T(8,128)(2,1)S(1)}, s32[]{:T(128)}, /*index=5*/s32[]{:T(128)}) while((s32[]{:T(128)}, bf16[384,4096]{1,0:T(8,128)(2,1)}, s32[8,2]{0,1:T(2,128)S(1)}, bf16[8,1,3456]{2,0,1:T(8,128)(2,1)S(1)}, s32[]{:T(128)}, /*index=5*/s32[]{:T(128)}) %tuple.81), condition=%wide.while_cond, body=%wide.while_body.sunk | while | flops 2 | bytes 27765 | solution.py:46
  329.3 2.3 reshape.278
  334.0 23.5 %while.20 = (s32[]{:T(128)}, f32[384,3797]{1,0:T(8,128)}, s32[8,2]{0,1:T(2,128)S(1)}, f32[8,1,3072]{2,1,0:T(1,128)S(1)}, s32[]{:T(128)}) while((s32[]{:T(128)}, f32[384,3797]{1,0:T(8,128)}, s32[8,2]{0,1:T(2,128)S(1)}, f32[8,1,3072]{2,1,0:T(1,128)S(1)}, s32[]{:T(128)}) %tuple.84), condition=%wide.while_cond.1, body=%wide.while_body.1.sunk | while | flops 2 | bytes 24685 | solution.py:47
  362.2 24.4 %while.19 = (s32[]{:T(128)}, bf16[384,4096]{1,0:T(8,128)(2,1)}, s32[8,2]{0,1:T(2,128)S(1)}, bf16[8,1,3456]{2,0,1:T(8,128)(2,1)S(1)}, s32[]{:T(128)}, /*index=5*/s32[]{:T(128)}) while((s32[]{:T(128)}, bf16[384,4096]{1,0:T(8,128)(2,1)}, s32[8,2]{0,1:T(2,128)S(1)}, bf16[8,1,3456]{2,0,1:T(8,128)(2,1)S(1)}, s32[]{:T(128)}, /*index=5*/s32[]{:T(128)}) %tuple.81), condition=%wide.while_cond, body=%wide.while_body.sunk | while | flops 2 | bytes 27765 | solution.py:46
  387.0 2.3 reshape.278
  391.7 23.5 %while.20 = (s32[]{:T(128)}, f32[384,3797]{1,0:T(8,128)}, s32[8,2]{0,1:T(2,128)S(1)}, f32[8,1,3072]{2,1,0:T(1,128)S(1)}, s32[]{:T(128)}) while((s32[]{:T(128)}, f32[384,3797]{1,0:T(8,128)}, s32[8,2]{0,1:T(2,128)S(1)}, f32[8,1,3072]{2,1,0:T(1,128)S(1)}, s32[]{:T(128)}) %tuple.84), condition=%wide.while_cond.1, body=%wide.while_body.1.sunk | while | flops 2 | bytes 24685 | solution.py:47
  419.9 24.4 %while.19 = (s32[]{:T(128)}, bf16[384,4096]{1,0:T(8,128)(2,1)}, s32[8,2]{0,1:T(2,128)S(1)}, bf16[8,1,3456]{2,0,1:T(8,128)(2,1)S(1)}, s32[]{:T(128)}, /*index=5*/s32[]{:T(128)}) while((s32[]{:T(128)}, bf16[384,4096]{1,0:T(8,128)(2,1)}, s32[8,2]{0,1:T(2,128)S(1)}, bf16[8,1,3456]{2,0,1:T(8,128)(2,1)S(1)}, s32[]{:T(128)}, /*index=5*/s32[]{:T(128)}) %tuple.81), condition=%wide.while_cond, body=%wide.while_body.sunk | while | flops 2 | bytes 27765 | solution.py:46
  444.7 2.3 reshape.278
  449.5 23.5 %while.20 = (s32[]{:T(128)}, f32[384,3797]{1,0:T(8,128)}, s32[8,2]{0,1:T(2,128)S(1)}, f32[8,1,3072]{2,1,0:T(1,128)S(1)}, s32[]{:T(128)}) while((s32[]{:T(128)}, f32[384,3797]{1,0:T(8,128)}, s32[8,2]{0,1:T(2,128)S(1)}, f32[8,1,3072]{2,1,0:T(1,128)S(1)}, s32[]{:T(128)}) %tuple.84), condition=%wide.while_cond.1, body=%wide.while_body.1.sunk | while | flops 2 | bytes 24685 | solution.py:47
  477.7 24.4 %while.19 = (s32[]{:T(128)}, bf16[384,4096]{1,0:T(8,128)(2,1)}, s32[8,2]{0,1:T(2,128)S(1)}, bf16[8,1,3456]{2,0,1:T(8,128)(2,1)S(1)}, s32[]{:T(128)}, /*index=5*/s32[]{:T(128)}) while((s32[]{:T(128)}, bf16[384,4096]{1,0:T(8,128)(2,1)}, s32[8,2]{0,1:T(2,128)S(1)}, bf16[8,1,3456]{2,0,1:T(8,128)(2,1)S(1)}, s32[]{:T(128)}, /*index=5*/s32[]{:T(128)}) %tuple.81), condition=%wide.while_cond, body=%wide.while_body.sunk | while | flops 2 | bytes 27765 | solution.py:46
  502.4 2.3 reshape.278
  507.2 23.5 %while.20 = (s32[]{:T(128)}, f32[384,3797]{1,0:T(8,128)}, s32[8,2]{0,1:T(2,128)S(1)}, f32[8,1,3072]{2,1,0:T(1,128)S(1)}, s32[]{:T(128)}) while((s32[]{:T(128)}, f32[384,3797]{1,0:T(8,128)}, s32[8,2]{0,1:T(2,128)S(1)}, f32[8,1,3072]{2,1,0:T(1,128)S(1)}, s32[]{:T(128)}) %tuple.84), condition=%wide.while_cond.1, body=%wide.while_body.1.sunk | while | flops 2 | bytes 24685 | solution.py:47
  533.4 11.2 %all_to_all.5 = f32[8,1,3072]{2,1,0:T(1,128)S(1)} all-to-all(f32[8,1,3072]{2,1,0:T(1,128)S(1)} %reshape.182), channel_id=1, replica_groups=mesh['span'=2,'tmpl'=2,'stn'=8] {'stn'}, dimensions={0} | all-to-all | bytes 196608 | tf_op jit(solution)/shard_map/all_to_all | solution.py:112
  (642 shorter events, 372.7 us)
Async XLA Ops:
  0.0 5.2 copy-start
  0.0 37.7 %collective-permute-start = (bf16[384,2048]{1,0:T(8,128)(2,1)}, bf16[384,2048]{1,0:T(8,128)(2,1)}, u32[]{:S(2)}, u32[]{:S(2)}) collective-permute-start(bf16[384,2048]{1,0:T(8,128)(2,1)} %param.7), channel_id=1, source_target_pairs={{0,8},{8,0},{1,9},{9,1},{2,10},{10,2},{3,11},{11,3},{4,12},{12,4},... | collective-permute-start | bytes 4718600 | tf_op jit(solution)/shard_map/ppermute | solution.py:21
  60.1 6.6 %copy-start.1 = (bf16[384,2048]{1,0:T(8,128)(2,1)S(1)}, bf16[384,2048]{1,0:T(8,128)(2,1)}, u32[]{:S(2)}) copy-start(bf16[384,2048]{1,0:T(8,128)(2,1)} %param.7) | copy-start | bytes 4718596
